TPU v7x, 512 devices: a whole 4x8x8 slice. The times are simulated.
512 devices in a mesh: tm: 64 (over z, y), state: 8 (over x, core).
Axes of the slice: x: 4, y: 8, z: 8, core: 2. Of those that a mesh axis runs over, the one named last changes fastest.
Arguments:
- offsets: int32 [5], replicated, may hold values from -3 to 3
- coefficients: float32 [5, 2048], replicated, may hold values from 0.1 to 1
- gain_matrix: bfloat16 [64, 1, 2048, 512], P('tm', None, 'state'), may hold values from -0.0625 to 0.0625
- direct_gain: float32 [64, 1, 512], P('tm'), may hold values from 0.2 to 0.8
- observed_cells: int32 [64, 1, 512], P('tm'), may hold values from 0 to 2047
- observed_values: float32 [64, 1, 512], P('tm'), may hold values from -4 to 4
Outputs:
- transition: float32 [64, 2048, 2048], P('tm', None, 'state')
- offset_term: float32 [64, 2048], P('tm')
All inputs are finite; a program needn't handle non-finite values.
Results may differ from a plain program's by a relative error of at most 0.0036.
Values may be sent and summed in bfloat16 or wider, within the bound.
A program may use at most 64 MiB of HBM per device.

v0:
```python
import jax
import jax.numpy as jnp
from jax import lax
from jax.sharding import PartitionSpec as P


def from_behind(value, axis, steps):
    count = lax.axis_size(axis)
    leading, last = (max(0, -steps), min(count, count - steps))
    return lax.ppermute(value, axis, [(source, source + steps) for source in range(leading, last)])


def advance(matrix, step_gains, cells_used, weights, offsets, forcing):
    spread = weights[0][:, None] * jnp.roll(matrix, -offsets[0], axis=0)
    for tap_index in range(1, weights.shape[0]):
        spread = spread + weights[tap_index][:, None] * jnp.roll(
            matrix, -offsets[tap_index], axis=0
        )
    picked = jnp.take(spread, cells_used[0], axis=0)
    if forcing is not None:
        picked = picked - forcing[0][:, None]
    correction = jnp.dot(
        step_gains[0], picked.astype(jnp.bfloat16), preferred_element_type=jnp.float32
    )
    matrix = spread - correction
    return matrix


def local_gain_rows(gain_matrix, direct_gain, observed_cells):
    row_count = gain_matrix.shape[2]
    first_row = lax.axis_index("state") * row_count
    cell_ids = first_row + lax.broadcasted_iota(jnp.int32, gain_matrix.shape[1:], 1)
    observed_hit = cell_ids == observed_cells[0][:, None, :]
    extra = jnp.where(
        observed_hit, direct_gain[0][:, None, :], jnp.zeros_like(direct_gain[0][:, None, :])
    )
    return (gain_matrix[0].astype(jnp.float32) + extra).astype(jnp.bfloat16)


def shards(offsets, coefficients, gain_matrix, direct_gain, observed_cells, observed_values):
    weights = coefficients / jnp.sum(coefficients, axis=0, keepdims=True)
    gain_rows = local_gain_rows(gain_matrix, direct_gain, observed_cells)
    gain_full = lax.all_gather(gain_rows, "state", axis=1, tiled=True)
    cells_used = observed_cells[0]
    forcing = observed_values[0]
    cell_count = gain_full.shape[1]
    columns = gain_rows.shape[1]
    first_column = lax.axis_index("state") * columns
    row_ids = lax.broadcasted_iota(jnp.int32, (cell_count, columns), 0)
    column_ids = first_column + lax.broadcasted_iota(jnp.int32, (cell_count, columns), 1)
    identity_panel = (row_ids == column_ids).astype(jnp.float32)
    span_index = lax.axis_index("tm")

    def own_map(matrix, forced_values=None):
        return advance(matrix, gain_full, cells_used, weights, offsets, forced_values)

    level_zero_trans = own_map(identity_panel)
    level_zero_shift = own_map(jnp.zeros((cell_count, 1), jnp.float32), forcing)
    left_trans, left_shift = from_behind((level_zero_trans, level_zero_shift), "tm", 1)
    level_one_trans = jnp.where(span_index >= 1, own_map(left_trans), level_zero_trans)
    level_one_shift = jnp.where(
        span_index >= 1, own_map(left_shift) + level_zero_shift, level_zero_shift
    )
    far_trans, far_shift = from_behind((level_one_trans, level_one_shift), "tm", 2)
    far_trans = jnp.where(span_index == 1, identity_panel, far_trans)
    earlier_gains, earlier_cells = from_behind((gain_full, cells_used), "tm", 1)
    carried_trans = own_map(
        advance(far_trans, earlier_gains, earlier_cells, weights, offsets, None)
    )
    carried_shift = own_map(
        advance(far_shift, earlier_gains, earlier_cells, weights, offsets, None)
    )
    first_carried = 1
    transition = jnp.where(span_index >= first_carried, carried_trans, level_one_trans)
    offset_term = jnp.where(span_index >= 2, carried_shift + level_one_shift, level_one_shift)
    return (transition[None], offset_term[:, 0][None])


def solution(mesh):
    in_specs = (
        P(),
        P(),
        P("tm", None, "state", None),
        P("tm", None, None),
        P("tm", None, None),
        P("tm", None, None),
    )
    out_specs = (P("tm", None, "state"), P("tm", None))
    return jax.shard_map(shards, mesh=mesh, in_specs=in_specs, out_specs=out_specs, check_vma=False)
```

profile of v0, /device:TPU:24, one launch (start us, length us, event | category | flops | bytes accessed | tf_op | source)
XLA Modules:
  0.0 283.7 jit_solution(14787118618400152176)
XLA Ops:
  7.2 0.0 all-gather.2.cloned.1.call-start
  7.2 1.8 fusion.67
  9.1 0.0 all-gather.2.cloned.1.call-update
  9.1 4.7 %collective-permute-start.3 = (s32[1,512]{1,0:T(1,128)}, s32[1,512]{1,0:T(1,128)S(1)}, u32[]{:S(2)}, u32[]{:S(2)}) collective-permute-start(s32[1,512]{1,0:T(1,128)} %bitcast.144), channel_id=1, source_target_pairs={{0,8},{8,16},{16,24},{24,32},{32,40},{40,48},{48,56},{56,64},{64,7... | collective-permute-start | bytes 6152 | tf_op jit(solution)/shard_map/ppermute | solution.py:10
  13.8 1.5 fusion.131
  18.6 0.9 reduce_sum.9
  19.5 0.7 compare_select_fusion.1
  20.2 0.9 broadcast_divide_fusion
  21.1 0.2 fusion.66
  21.3 5.6 %fusion.42 = f32[2048,256]{1,0:T(8,128)S(1)} fusion(s32[]{:T(128)S(6)} %select_n.189, f32[2048,256]{1,0:T(8,128)S(1)} %fusion.66, s32[]{:T(128)S(6)} %select_n.181, s32[]{:T(128)S(6)} %select_n.183, s32[]{:T(128)S(6)} %select_n.185, s32[]{:T(128)S(6)} %select_n.187, f32[2048]{0:T(1024)S(1)} %bitcast.127, f32[2048]{0:T(1024)S(1)} %bitcast.131, ...), kind=kLoop, calls=%fused_computation.88 | loop fusion | flops 7340032 | bytes 4235284 | tf_op jit(solution)/shard_map/add | solution.py:16
  27.0 0.0 copy-start.1
  27.0 0.0 copy-start.2
  27.0 1.6 gather_fusion
  28.6 0.4 fusion.89
  28.9 3.1 %gather_fusion.4 = f32[512]{0:T(512)S(1)} fusion(f32[2048]{0:T(1024)S(1)} %bitcast.119, s32[1024]{0:T(1024)S(1)} %pad_clamp_fusion.1), kind=kCustom, calls=%fused_computation.1.clone | custom fusion | bytes 6144 | tf_op jit(solution)/shard_map/jit(_take)/gather | solution.py:19
  32.1 12.9 %all-gather.2.cloned.1.call-done = bf16[1,2048,512]{2,1,0:T(8,128)(2,1)} async-done(((bf16[1,256,512]{2,1,0:T(8,128)(2,1)}), bf16[1,2048,512]{2,1,0:T(8,128)(2,1)}) %all-gather.2.cloned.1.call-update) | async-done | bytes 2097168 | tf_op jit(solution)/shard_map/all_gather | solution.py:43
  45.1 4.5 %convolution_subtract_fusion.3 = f32[2048,256]{1,0:T(8,128)} fusion(f32[2048,256]{1,0:T(8,128)} %copy-done.1, bf16[1,2048,512]{2,1,0:T(8,128)(2,1)} %all-gather.2.cloned.1.call-done, bf16[512,256]{1,0:T(8,128)(2,1)S(1)} %gather_fusion, pred[512]{0:T(512)(128)(4,1)S(1)} %get-tuple-element.9), kind=kOutput, calls=%fused_computation.43 | convolution fusion | flops 537526272 | bytes 6554112 | tf_op jit(solution)/shard_map/dot_general | solution.py:22
  49.6 4.6 %collective-permute-start = (f32[2048,256]{1,0:T(8,128)}, f32[2048,256]{1,0:T(8,128)}, u32[]{:S(2)}, u32[]{:S(2)}) collective-permute-start(f32[2048,256]{1,0:T(8,128)} %convolution_subtract_fusion.3), channel_id=1, source_target_pairs={{0,8},{8,16},{16,24},{24,32},{32,40},{40,48},{48,56},{56,64},{64,7... | collective-permute-start | bytes 6291464 | tf_op jit(solution)/shard_map/ppermute | solution.py:10
  54.2 0.6 fusion.11
  54.8 2.5 collective-permute-start.4
  57.3 0.0 collective-permute-done.3
  57.4 42.5 %collective-permute-done.4 = f32[2048,1]{0,1:T(1,128)S(1)} collective-permute-done((f32[2048,1]{0,1:T(1,128)S(1)}, f32[2048,1]{0,1:T(1,128)S(1)}, u32[]{:S(2)}, u32[]{:S(2)}) %collective-permute-start.4) | collective-permute-done | bytes 8224 | tf_op jit(solution)/shard_map/ppermute | solution.py:10
  99.9 0.2 fusion.92
  100.0 3.1 %gather_fusion.5 = f32[512]{0:T(512)S(1)} fusion(f32[2048]{0:T(1024)S(1)} %bitcast.122, s32[1024]{0:T(1024)S(1)} %pad_clamp_fusion.1), kind=kCustom, calls=%fused_computation.5.clone | custom fusion | bytes 6144 | tf_op jit(solution)/shard_map/jit(_take)/gather | solution.py:19
  103.2 0.6 fusion.10
  103.8 4.4 %collective-permute-start.5 = (f32[2048,1]{0,1:T(1,128)S(1)}, f32[2048,1]{0,1:T(1,128)S(1)}, u32[]{:S(2)}, u32[]{:S(2)}) collective-permute-start(f32[2048,1]{0,1:T(1,128)S(1)} %fusion.10), channel_id=1, source_target_pairs={{0,16},{8,24},{16,32},{24,40},{32,48},{40,56},{48,64},{56,72},{64,... | collective-permute-start | bytes 24584 | tf_op jit(solution)/shard_map/ppermute | solution.py:10
  108.3 3.1 %collective-permute-start.2 = (bf16[1,2048,512]{2,1,0:T(8,128)(2,1)S(1)}, bf16[1,2048,512]{2,1,0:T(8,128)(2,1)}, u32[]{:S(2)}, u32[]{:S(2)}) collective-permute-start(bf16[1,2048,512]{2,1,0:T(8,128)(2,1)S(1)} %copy-done), channel_id=1, source_target_pairs={{0,8},{8,16},{16,24},{24,32},{32,40},{40,48},{48,56},{56,64},{64,7... | collective-permute-start | bytes 6291464 | tf_op jit(solution)/shard_map/ppermute | solution.py:10
  111.4 1.7 constant_dynamic-update-slice_fusion.1
  113.2 1.7 constant_dynamic-update-slice_fusion
  114.9 3.1 %fusion.62 = f32[2048,256]{1,0:T(8,128)} fusion(f32[4096,256]{1,0:T(8,128)S(1)} %constant_dynamic-update-slice_fusion, s32[]{:T(128)S(6)} %select_n.189, s32[]{:T(128)S(6)} %select_n.187, s32[]{:T(128)S(6)} %select_n.185, s32[]{:T(128)S(6)} %select_n.183, s32[]{:T(128)S(6)} %select_n.181, f32[2048]{0:T(1024)S(1)} %bitcast.128, f32[2048]{0:T(1024)S(1)} %bitcast.132, ...), kind=kLoop, calls=%fused_computation.109 | loop fusion | flops 4718592 | bytes 12623892 | tf_op jit(solution)/shard_map/add | solution.py:16
  118.0 3.1 %gather_fusion.1 = bf16[512,256]{1,0:T(8,128)(2,1)S(1)} fusion(f32[2048,256]{1,0:T(8,128)} %fusion.62, s32[1024]{0:T(1024)S(1)} %pad_clamp_fusion.1), kind=kCustom, calls=%fused_computation.2.clone | custom fusion | bytes 526336 | tf_op jit(solution)/shard_map/jit(_take)/gather | solution.py:19
  121.1 3.7 %fusion.1 = f32[2048,256]{1,0:T(8,128)} fusion(f32[2048,256]{1,0:T(8,128)} %convolution_subtract_fusion.3, f32[2048,256]{1,0:T(8,128)} %fusion.62, bf16[1,2048,512]{2,1,0:T(8,128)(2,1)S(1)} %copy-done, pred[]{:T(512)S(6)} %ge.18, bf16[512,256]{1,0:T(8,128)(2,1)S(1)} %gather_fusion.1, pred[512]{0:T(512)(128)(4,1)S(1)} %get-tuple-element.9), kind=kOutput, calls=%fused_computation.42 | convolution fusion | flops 538050560 | bytes 8651265 | tf_op jit(solution)/shard_map/dot_general | solution.py:22
  124.9 5.1 %collective-permute-start.1 = (f32[2048,256]{1,0:T(8,128)}, f32[2048,256]{1,0:T(8,128)}, u32[]{:S(2)}, u32[]{:S(2)}) collective-permute-start(f32[2048,256]{1,0:T(8,128)} %fusion.1), channel_id=1, source_target_pairs={{0,16},{8,24},{16,32},{24,40},{32,48},{40,56},{48,64},{56,72},{64,... | collective-permute-start | bytes 6291464 | tf_op jit(solution)/shard_map/ppermute | solution.py:10
  130.0 0.2 fusion.94
  130.1 3.1 %gather_fusion.6 = f32[512]{0:T(512)S(1)} fusion(f32[2048]{0:T(1024)S(1)} %bitcast.120, s32[1024]{0:T(1024)S(1)} %pad_clamp_fusion), kind=kCustom, calls=%fused_computation.6.clone | custom fusion | bytes 6144 | tf_op jit(solution)/shard_map/jit(_take)/gather | solution.py:19
  133.3 26.4 %collective-permute-done.2 = bf16[1,2048,512]{2,1,0:T(8,128)(2,1)} collective-permute-done((bf16[1,2048,512]{2,1,0:T(8,128)(2,1)S(1)}, bf16[1,2048,512]{2,1,0:T(8,128)(2,1)}, u32[]{:S(2)}, u32[]{:S(2)}) %collective-permute-start.2) | collective-permute-done | bytes 2097184 | tf_op jit(solution)/shard_map/ppermute | solution.py:10
  159.7 2.2 fusion.7
  161.9 0.4 fusion.97
  162.3 3.1 %gather_fusion.7 = f32[512]{0:T(512)S(1)} fusion(f32[2048]{0:T(1024)S(1)} %bitcast.121, s32[1024]{0:T(1024)S(1)} %pad_clamp_fusion.1), kind=kCustom, calls=%fused_computation.7.clone | custom fusion | bytes 6144 | tf_op jit(solution)/shard_map/jit(_take)/gather | solution.py:19
  165.5 1.3 fusion.6
  166.7 82.3 %collective-permute-done.1 = f32[2048,256]{1,0:T(8,128)} collective-permute-done((f32[2048,256]{1,0:T(8,128)}, f32[2048,256]{1,0:T(8,128)}, u32[]{:S(2)}, u32[]{:S(2)}) %collective-permute-start.1) | collective-permute-done | bytes 2097184 | tf_op jit(solution)/shard_map/ppermute | solution.py:10
  249.0 1.9 broadcast_select_fusion
  250.9 6.4 %fusion.28 = f32[2048,256]{1,0:T(8,128)} fusion(s32[]{:T(128)S(6)} %select_n.189, f32[2048,256]{1,0:T(8,128)S(1)} %broadcast_select_fusion, s32[]{:T(128)S(6)} %select_n.181, s32[]{:T(128)S(6)} %select_n.183, s32[]{:T(128)S(6)} %select_n.185, s32[]{:T(128)S(6)} %select_n.187, f32[2048]{0:T(1024)S(1)} %bitcast.129, f32[2048]{0:T(1024)S(1)} %bitcast.133, ...), kind=kLoop, calls=%fused_computation.74 | loop fusion | flops 7340032 | bytes 4235284 | tf_op jit(solution)/shard_map/add | solution.py:16
  257.3 3.1 %gather_fusion.2 = bf16[512,256]{1,0:T(8,128)(2,1)S(1)} fusion(f32[2048,256]{1,0:T(8,128)} %fusion.28, s32[1024]{0:T(1024)S(1)} %pad_clamp_fusion), kind=kCustom, calls=%fused_computation.3.clone | custom fusion | bytes 526336 | tf_op jit(solution)/shard_map/jit(_take)/gather | solution.py:19
  260.5 3.0 %convolution_subtract_fusion.1 = f32[2048,256]{1,0:T(8,128)S(1)} fusion(f32[2048,256]{1,0:T(8,128)} %fusion.28, bf16[1,2048,512]{2,1,0:T(8,128)(2,1)} %collective-permute-done.2, bf16[512,256]{1,0:T(8,128)(2,1)S(1)} %gather_fusion.2, pred[512]{0:T(512)(128)(4,1)S(1)} %get-tuple-element.6), kind=kOutput, calls=%fused_computation.40 | convolution fusion | flops 537526272 | bytes 6554112 | tf_op jit(solution)/shard_map/dot_general | solution.py:22
  263.5 6.4 %fusion.14 = f32[2048,256]{1,0:T(8,128)} fusion(s32[]{:T(128)S(6)} %select_n.189, f32[2048,256]{1,0:T(8,128)S(1)} %convolution_subtract_fusion.1, s32[]{:T(128)S(6)} %select_n.181, s32[]{:T(128)S(6)} %select_n.183, s32[]{:T(128)S(6)} %select_n.185, s32[]{:T(128)S(6)} %select_n.187, f32[2048]{0:T(1024)S(1)} %bitcast.130, f32[2048]{0:T(1024)S(1)} %bitcast.134, ...), kind=kLoop, calls=%fused_computation.60 | loop fusion | flops 7340032 | bytes 4235284 | tf_op jit(solution)/shard_map/add | solution.py:16
  270.0 3.1 %gather_fusion.3 = bf16[512,256]{1,0:T(8,128)(2,1)S(1)} fusion(f32[2048,256]{1,0:T(8,128)} %fusion.14, s32[1024]{0:T(1024)S(1)} %pad_clamp_fusion.1), kind=kCustom, calls=%fused_computation.4.clone | custom fusion | bytes 526336 | tf_op jit(solution)/shard_map/jit(_take)/gather | solution.py:19
  273.1 3.7 %fusion.2 = f32[1,2048,256]{2,1,0:T(8,128)} fusion(f32[2048,256]{1,0:T(8,128)} %fusion.1, f32[2048,256]{1,0:T(8,128)} %fusion.14, bf16[1,2048,512]{2,1,0:T(8,128)(2,1)S(1)} %copy-done, pred[]{:T(512)S(6)} %ge.18, bf16[512,256]{1,0:T(8,128)(2,1)S(1)} %gather_fusion.3, pred[512]{0:T(512)(128)(4,1)S(1)} %get-tuple-element.9), kind=kOutput, calls=%fused_computation.44 | convolution fusion | flops 538050560 | bytes 8651265 | tf_op jit(solution)/shard_map/dot_general | solution.py:22
  (22 shorter events, 0.1 us)
Async XLA Ops:
  7.2 37.9 %all-gather.2.cloned.1.call-start = ((), (), s32[]{:S(2)}) async-start(), calls=%async_computation | async-start | bytes 2359296 | tf_op jit(solution)/shard_map/all_gather | solution.py:43
  9.1 48.3 %collective-permute-start.3 = (s32[1,512]{1,0:T(1,128)}, s32[1,512]{1,0:T(1,128)S(1)}, u32[]{:S(2)}, u32[]{:S(2)}) collective-permute-start(s32[1,512]{1,0:T(1,128)} %bitcast.144), channel_id=1, source_target_pairs={{0,8},{8,16},{16,24},{24,32},{32,40},{40,48},{48,56},{56,64},{64,7... | collective-permute-start | bytes 6152 | tf_op jit(solution)/shard_map/ppermute | solution.py:10
  27.0 5.1 %copy-start.1 = (f32[2048,256]{1,0:T(8,128)}, f32[2048,256]{1,0:T(8,128)S(1)}, u32[]{:S(2)}) copy-start(f32[2048,256]{1,0:T(8,128)S(1)} %fusion.42) | copy-start | bytes 6291460
  27.0 5.1 %copy-start.2 = (s32[1,1,512]{2,1,0:T(1,128)S(1)}, s32[1,1,512]{2,1,0:T(1,128)}, u32[]{:S(2)}) copy-start(s32[1,1,512]{2,1,0:T(1,128)} %param.18) | copy-start | bytes 6148
  45.0 9.1 %copy-start = (bf16[1,2048,512]{2,1,0:T(8,128)(2,1)S(1)}, bf16[1,2048,512]{2,1,0:T(8,128)(2,1)}, u32[]{:S(2)}) copy-start(bf16[1,2048,512]{2,1,0:T(8,128)(2,1)} %all-gather.2.cloned.1.call-done) | copy-start | bytes 6291460
  45.1 9.1 %copy-start.3 = (f32[1,1,512]{2,1,0:T(1,128)S(1)}, f32[1,1,512]{2,1,0:T(1,128)}, u32[]{:S(2)}) copy-start(f32[1,1,512]{2,1,0:T(1,128)} %param.19) | copy-start | bytes 6148
  49.6 61.9 %collective-permute-start = (f32[2048,256]{1,0:T(8,128)}, f32[2048,256]{1,0:T(8,128)}, u32[]{:S(2)}, u32[]{:S(2)}) collective-permute-start(f32[2048,256]{1,0:T(8,128)} %convolution_subtract_fusion.3), channel_id=1, source_target_pairs={{0,8},{8,16},{16,24},{24,32},{32,40},{40,48},{48,56},{56,64},{64,7... | collective-permute-start | bytes 6291464 | tf_op jit(solution)/shard_map/ppermute | solution.py:10
  54.8 45.0 %collective-permute-start.4 = (f32[2048,1]{0,1:T(1,128)S(1)}, f32[2048,1]{0,1:T(1,128)S(1)}, u32[]{:S(2)}, u32[]{:S(2)}) collective-permute-start(f32[2048,1]{0,1:T(1,128)S(1)} %fusion.11), channel_id=1, source_target_pairs={{0,8},{8,16},{16,24},{24,32},{32,40},{40,48},{48,56},{56,64},{64,7... | collective-permute-start | bytes 24584 | tf_op jit(solution)/shard_map/ppermute | solution.py:10
  103.8 7.6 %collective-permute-start.5 = (f32[2048,1]{0,1:T(1,128)S(1)}, f32[2048,1]{0,1:T(1,128)S(1)}, u32[]{:S(2)}, u32[]{:S(2)}) collective-permute-start(f32[2048,1]{0,1:T(1,128)S(1)} %fusion.10), channel_id=1, source_target_pairs={{0,16},{8,24},{16,32},{24,40},{32,48},{40,56},{48,64},{56,72},{64,... | collective-permute-start | bytes 24584 | tf_op jit(solution)/shard_map/ppermute | solution.py:10
  108.3 51.4 %collective-permute-start.2 = (bf16[1,2048,512]{2,1,0:T(8,128)(2,1)S(1)}, bf16[1,2048,512]{2,1,0:T(8,128)(2,1)}, u32[]{:S(2)}, u32[]{:S(2)}) collective-permute-start(bf16[1,2048,512]{2,1,0:T(8,128)(2,1)S(1)} %copy-done), channel_id=1, source_target_pairs={{0,8},{8,16},{16,24},{24,32},{32,40},{40,48},{48,56},{56,64},{64,7... | collective-permute-start | bytes 6291464 | tf_op jit(solution)/shard_map/ppermute | solution.py:10
  124.9 124.1 %collective-permute-start.1 = (f32[2048,256]{1,0:T(8,128)}, f32[2048,256]{1,0:T(8,128)}, u32[]{:S(2)}, u32[]{:S(2)}) collective-permute-start(f32[2048,256]{1,0:T(8,128)} %fusion.1), channel_id=1, source_target_pairs={{0,16},{8,24},{16,32},{24,40},{32,48},{40,56},{48,64},{56,72},{64,... | collective-permute-start | bytes 6291464 | tf_op jit(solution)/shard_map/ppermute | solution.py:10
Sparse Core Ops, SparseCore 0:
  10.1 34.8 all-gather.1
where the time goes:
time: 284 us
  waiting for transfers between devices  164 us (58%)
  other arithmetic  29.1 us (10%)
  local copies, waits for them, and re-layouts  28.6 us (10%)
  starting transfers between devices  24.4 us (9%)
  matrix products  19.8 us (7%)
  between operations  17.7 us (6%)
    ppermute x6, waiting for transfers between devices, from_behind(): lax.ppermute(value, axis, [(source, source + steps) for source in range(l...  151 us
    ppermute x6, starting transfers between devices, from_behind(): lax.ppermute(value, axis, [(source, source + steps) for source in range(l...  24.4 us
    gather x8, local copies, waits for them, and re-layouts, advance(): picked = jnp.take(spread, cells_used[0], axis=0)  23.6 us
    add x8, other arithmetic, advance(): spread + weights[tap_index][:, None] * jnp.roll(matrix, -offsets[tap_inde...  22.7 us
    dot_general x8, matrix products, advance(): jnp.dot(step_gains[0], picked.astype(jnp.bfloat16), preferred_element_typ...  19.8 us
    all_gather x1, waiting for transfers between devices, shards(): gain_full = lax.all_gather(gain_rows, 'state', axis=1, tiled=True)  12.9 us
  transfers between devices with their start and end apart: 7, of which 4 were waited for; matrix products, arithmetic and copies ran while one was open for 17% of the time, Pallas kernels for 0%

commit v1 on v0

--- a/solution.py
+++ b/solution.py
@@ -40,7 +40,9 @@
 def shards(offsets, coefficients, gain_matrix, direct_gain, observed_cells, observed_values):
     weights = coefficients / jnp.sum(coefficients, axis=0, keepdims=True)
     gain_rows = local_gain_rows(gain_matrix, direct_gain, observed_cells)
-    gain_full = lax.all_gather(gain_rows, "state", axis=1, tiled=True)
+    gain_full = jnp.concatenate(
+        lax.all_to_all(jnp.stack([gain_rows] * lax.axis_size("state")), "state", 0, 0), axis=1
+    )
     cells_used = observed_cells[0]
     forcing = observed_values[0]
     cell_count = gain_full.shape[1]

time: 284 us -> 268 us (0.944)
  the two profiles are of different devices: /device:TPU:24 before, /device:TPU:248 now
where the time goes in v1:
time: 268 us; the launch traced here: 267 us
  waiting for transfers between devices  153 us (57%)
  starting transfers between devices  33.3 us (12%)
  local copies, waits for them, and re-layouts  30.8 us (11%)
  other arithmetic  26.8 us (10%)
  matrix products  19 us (7%)
  between operations  4.17 us (2%)
    ppermute x6, waiting for transfers between devices, from_behind(): lax.ppermute(value, axis, [(source, source + steps) for source in range(l...  148 us
    ppermute x6, starting transfers between devices, from_behind(): lax.ppermute(value, axis, [(source, source + steps) for source in range(l...  28.9 us
    gather x8, local copies, waits for them, and re-layouts, advance(): picked = jnp.take(spread, cells_used[0], axis=0)  25.2 us
    add x8, other arithmetic, advance(): spread + weights[tap_index][:, None] * jnp.roll(matrix, -offsets[tap_inde...  23.5 us
    dot_general x8, matrix products, advance(): jnp.dot(step_gains[0], picked.astype(jnp.bfloat16), preferred_element_typ...  19 us
  transfers between devices with their start and end apart: 7, of which 4 were waited for; matrix products, arithmetic and copies ran while one was open for 17% of the time, Pallas kernels for 0%

profile of v1, /device:TPU:248, one launch (start us, length us, event | category | flops | bytes accessed | tf_op | source)
XLA Modules:
  0.0 266.8 jit_solution(9194665640963868079)
XLA Ops:
  0.6 1.1 fusion.61
  1.8 1.5 stack.5
  3.3 4.4 %all-to-all-start = ((bf16[8,1,256,512]{3,2,1,0:T(8,128)(2,1)}), bf16[8,1,256,512]{3,2,1,0:T(8,128)(2,1)S(1)}, u32[]{:S(2)}, u32[]{:S(2)}) async-start(bf16[8,1,256,512]{3,2,1,0:T(8,128)(2,1)} %stack.5), calls=%async_computation | async-start | bytes 4194304 | tf_op jit(solution)/shard_map/all_to_all | solution.py:44
  7.7 0.0 copy-done.1
  7.7 4.7 %collective-permute-start.3 = (s32[1,512]{1,0:T(1,128)S(1)}, s32[1,512]{1,0:T(1,128)S(1)}, u32[]{:S(2)}, u32[]{:S(2)}) collective-permute-start(s32[1,512]{1,0:T(1,128)S(1)} %bitcast.145), channel_id=1, source_target_pairs={{0,8},{8,16},{16,24},{24,32},{32,40},{40,48},{48,56},{56,64},{64,7... | collective-permute-start | bytes 6152 | tf_op jit(solution)/shard_map/ppermute | solution.py:10
  12.4 0.0 copy-done
  12.5 0.0 copy-done.2
  12.5 0.6 fusion.125
  16.4 0.2 fusion.60
  16.6 6.4 %fusion.42 = f32[2048,256]{1,0:T(8,128)} fusion(s32[]{:T(128)S(6)} %select_n.190, f32[2048,256]{1,0:T(8,128)S(1)} %fusion.60, s32[]{:T(128)S(6)} %select_n.182, s32[]{:T(128)S(6)} %select_n.184, s32[]{:T(128)S(6)} %select_n.186, s32[]{:T(128)S(6)} %select_n.188, f32[2048]{0:T(1024)S(1)} %bitcast.128, f32[2048]{0:T(1024)S(1)} %bitcast.132, ...), kind=kLoop, calls=%fused_computation.88 | loop fusion | flops 7340032 | bytes 4235284 | tf_op jit(solution)/shard_map/add | solution.py:16
  23.0 3.1 %gather_fusion = bf16[512,256]{1,0:T(8,128)(2,1)S(1)} fusion(f32[2048,256]{1,0:T(8,128)} %fusion.42, s32[1024]{0:T(1024)S(1)} %pad_clamp_fusion.1), kind=kCustom, calls=%fused_computation.clone | custom fusion | bytes 526336 | tf_op jit(solution)/shard_map/jit(_take)/gather | solution.py:19
  26.2 0.4 fusion.83
  26.6 3.1 %gather_fusion.4 = f32[512]{0:T(512)S(1)} fusion(f32[2048]{0:T(1024)S(1)} %bitcast.113, s32[1024]{0:T(1024)S(1)} %pad_clamp_fusion.1), kind=kCustom, calls=%fused_computation.1.clone | custom fusion | bytes 6144 | tf_op jit(solution)/shard_map/jit(_take)/gather | solution.py:19
  29.7 5.2 %all-to-all-done = bf16[8,1,256,512]{3,2,1,0:T(8,128)(2,1)S(1)} async-done(((bf16[8,1,256,512]{3,2,1,0:T(8,128)(2,1)}), bf16[8,1,256,512]{3,2,1,0:T(8,128)(2,1)S(1)}, u32[]{:S(2)}, u32[]{:S(2)}) %all-to-all-start) | async-done | bytes 2097184 | tf_op jit(solution)/shard_map/all_to_all | solution.py:44
  34.9 3.7 %convolution_subtract_fusion.3 = f32[2048,256]{1,0:T(8,128)} fusion(f32[2048,256]{1,0:T(8,128)} %fusion.42, bf16[2048,512]{1,0:T(8,128)(2,1)S(1)} %bitcast.117, bf16[512,256]{1,0:T(8,128)(2,1)S(1)} %gather_fusion, pred[512]{0:T(512)(128)(4,1)S(1)} %get-tuple-element.9), kind=kOutput, calls=%fused_computation.43 | convolution fusion | flops 537526272 | bytes 6554112 | tf_op jit(solution)/shard_map/dot_general | solution.py:22
  38.7 4.7 %collective-permute-start = (f32[2048,256]{1,0:T(8,128)}, f32[2048,256]{1,0:T(8,128)}, u32[]{:S(2)}, u32[]{:S(2)}) collective-permute-start(f32[2048,256]{1,0:T(8,128)} %convolution_subtract_fusion.3), channel_id=1, source_target_pairs={{0,8},{8,16},{16,24},{24,32},{32,40},{40,48},{48,56},{56,64},{64,7... | collective-permute-start | bytes 6291464 | tf_op jit(solution)/shard_map/ppermute | solution.py:10
  43.4 0.6 fusion.11
  44.0 3.5 %collective-permute-start.4 = (f32[2048,1]{0,1:T(1,128)S(1)}, f32[2048,1]{0,1:T(1,128)S(1)}, u32[]{:S(2)}, u32[]{:S(2)}) collective-permute-start(f32[2048,1]{0,1:T(1,128)S(1)} %fusion.11), channel_id=1, source_target_pairs={{0,8},{8,16},{16,24},{24,32},{32,40},{40,48},{48,56},{56,64},{64,7... | collective-permute-start | bytes 24584 | tf_op jit(solution)/shard_map/ppermute | solution.py:10
  47.5 0.0 collective-permute-done.3
  47.5 40.9 %collective-permute-done.4 = f32[2048,1]{0,1:T(1,128)S(1)} collective-permute-done((f32[2048,1]{0,1:T(1,128)S(1)}, f32[2048,1]{0,1:T(1,128)S(1)}, u32[]{:S(2)}, u32[]{:S(2)}) %collective-permute-start.4) | collective-permute-done | bytes 8224 | tf_op jit(solution)/shard_map/ppermute | solution.py:10
  88.4 0.2 fusion.86
  88.6 3.1 %gather_fusion.5 = f32[512]{0:T(512)S(1)} fusion(f32[2048]{0:T(1024)S(1)} %bitcast.116, s32[1024]{0:T(1024)S(1)} %pad_clamp_fusion.1), kind=kCustom, calls=%fused_computation.5.clone | custom fusion | bytes 6144 | tf_op jit(solution)/shard_map/jit(_take)/gather | solution.py:19
  91.8 0.6 fusion.10
  92.4 5.4 %collective-permute-start.5 = (f32[2048,1]{0,1:T(1,128)S(1)}, f32[2048,1]{0,1:T(1,128)S(1)}, u32[]{:S(2)}, u32[]{:S(2)}) collective-permute-start(f32[2048,1]{0,1:T(1,128)S(1)} %fusion.10), channel_id=1, source_target_pairs={{0,16},{8,24},{16,32},{24,40},{32,48},{40,56},{48,64},{56,72},{64,... | collective-permute-start | bytes 24584 | tf_op jit(solution)/shard_map/ppermute | solution.py:10
  97.8 4.2 %collective-permute-start.2 = (bf16[1,2048,512]{2,1,0:T(8,128)(2,1)S(1)}, bf16[1,2048,512]{2,1,0:T(8,128)(2,1)}, u32[]{:S(2)}, u32[]{:S(2)}) collective-permute-start(bf16[1,2048,512]{2,1,0:T(8,128)(2,1)S(1)} %bitcast.120), channel_id=1, source_target_pairs={{0,8},{8,16},{16,24},{24,32},{32,40},{40,48},{48,56},{56,64},{64,7... | collective-permute-start | bytes 6291464 | tf_op jit(solution)/shard_map/ppermute | solution.py:10
  102.1 0.0 collective-permute-done.5
  102.1 0.0 collective-permute-done
  102.1 1.7 constant_dynamic-update-slice_fusion.1
  103.8 1.7 constant_dynamic-update-slice_fusion
  105.6 3.1 %fusion.56 = f32[2048,256]{1,0:T(8,128)} fusion(f32[4096,256]{1,0:T(8,128)S(1)} %constant_dynamic-update-slice_fusion, s32[]{:T(128)S(6)} %select_n.190, s32[]{:T(128)S(6)} %select_n.188, s32[]{:T(128)S(6)} %select_n.186, s32[]{:T(128)S(6)} %select_n.184, s32[]{:T(128)S(6)} %select_n.182, f32[2048]{0:T(1024)S(1)} %bitcast.129, f32[2048]{0:T(1024)S(1)} %bitcast.133, ...), kind=kLoop, calls=%fused_computation.103 | loop fusion | flops 4718592 | bytes 12623892 | tf_op jit(solution)/shard_map/add | solution.py:16
  108.7 3.1 %gather_fusion.1 = bf16[512,256]{1,0:T(8,128)(2,1)S(1)} fusion(f32[2048,256]{1,0:T(8,128)} %fusion.56, s32[1024]{0:T(1024)S(1)} %pad_clamp_fusion.1), kind=kCustom, calls=%fused_computation.2.clone | custom fusion | bytes 526336 | tf_op jit(solution)/shard_map/jit(_take)/gather | solution.py:19
  111.8 3.7 %fusion.1 = f32[2048,256]{1,0:T(8,128)} fusion(f32[2048,256]{1,0:T(8,128)} %convolution_subtract_fusion.3, f32[2048,256]{1,0:T(8,128)} %fusion.56, bf16[2048,512]{1,0:T(8,128)(2,1)S(1)} %bitcast.121, pred[]{:T(512)S(6)} %ge.18, bf16[512,256]{1,0:T(8,128)(2,1)S(1)} %gather_fusion.1, pred[512]{0:T(512)(128)(4,1)S(1)} %get-tuple-element.9), kind=kOutput, calls=%fused_computation.42 | convolution fusion | flops 538050560 | bytes 8651265 | tf_op jit(solution)/shard_map/dot_general | solution.py:22
  115.6 6.3 %collective-permute-start.1 = (f32[2048,256]{1,0:T(8,128)}, f32[2048,256]{1,0:T(8,128)}, u32[]{:S(2)}, u32[]{:S(2)}) collective-permute-start(f32[2048,256]{1,0:T(8,128)} %fusion.1), channel_id=1, source_target_pairs={{0,16},{8,24},{16,32},{24,40},{32,48},{40,56},{48,64},{56,72},{64,... | collective-permute-start | bytes 6291464 | tf_op jit(solution)/shard_map/ppermute | solution.py:10
  121.9 0.2 fusion.88
  122.1 3.1 %gather_fusion.6 = f32[512]{0:T(512)S(1)} fusion(f32[2048]{0:T(1024)S(1)} %bitcast.114, s32[1024]{0:T(1024)S(1)} %pad_clamp_fusion), kind=kCustom, calls=%fused_computation.6.clone | custom fusion | bytes 6144 | tf_op jit(solution)/shard_map/jit(_take)/gather | solution.py:19
  125.3 67.1 %collective-permute-done.2 = bf16[1,2048,512]{2,1,0:T(8,128)(2,1)} collective-permute-done((bf16[1,2048,512]{2,1,0:T(8,128)(2,1)S(1)}, bf16[1,2048,512]{2,1,0:T(8,128)(2,1)}, u32[]{:S(2)}, u32[]{:S(2)}) %collective-permute-start.2) | collective-permute-done | bytes 2097184 | tf_op jit(solution)/shard_map/ppermute | solution.py:10
  192.3 2.2 fusion.7
  194.6 0.4 fusion.91
  195.0 3.1 %gather_fusion.7 = f32[512]{0:T(512)S(1)} fusion(f32[2048]{0:T(1024)S(1)} %bitcast.115, s32[1024]{0:T(1024)S(1)} %pad_clamp_fusion.1), kind=kCustom, calls=%fused_computation.7.clone | custom fusion | bytes 6144 | tf_op jit(solution)/shard_map/jit(_take)/gather | solution.py:19
  198.1 1.3 fusion.6
  199.4 39.6 %collective-permute-done.1 = f32[2048,256]{1,0:T(8,128)} collective-permute-done((f32[2048,256]{1,0:T(8,128)}, f32[2048,256]{1,0:T(8,128)}, u32[]{:S(2)}, u32[]{:S(2)}) %collective-permute-start.1) | collective-permute-done | bytes 2097184 | tf_op jit(solution)/shard_map/ppermute | solution.py:10
  239.0 1.9 broadcast_select_fusion
  240.9 6.4 %fusion.28 = f32[2048,256]{1,0:T(8,128)} fusion(s32[]{:T(128)S(6)} %select_n.190, f32[2048,256]{1,0:T(8,128)S(1)} %broadcast_select_fusion, s32[]{:T(128)S(6)} %select_n.182, s32[]{:T(128)S(6)} %select_n.184, s32[]{:T(128)S(6)} %select_n.186, s32[]{:T(128)S(6)} %select_n.188, f32[2048]{0:T(1024)S(1)} %bitcast.130, f32[2048]{0:T(1024)S(1)} %bitcast.134, ...), kind=kLoop, calls=%fused_computation.74 | loop fusion | flops 7340032 | bytes 4235284 | tf_op jit(solution)/shard_map/add | solution.py:16
  247.3 3.1 %gather_fusion.2 = bf16[512,256]{1,0:T(8,128)(2,1)S(1)} fusion(f32[2048,256]{1,0:T(8,128)} %fusion.28, s32[1024]{0:T(1024)S(1)} %pad_clamp_fusion), kind=kCustom, calls=%fused_computation.3.clone | custom fusion | bytes 526336 | tf_op jit(solution)/shard_map/jit(_take)/gather | solution.py:19
  250.4 3.0 %convolution_subtract_fusion.1 = f32[2048,256]{1,0:T(8,128)S(1)} fusion(f32[2048,256]{1,0:T(8,128)} %fusion.28, bf16[1,2048,512]{2,1,0:T(8,128)(2,1)} %collective-permute-done.2, bf16[512,256]{1,0:T(8,128)(2,1)S(1)} %gather_fusion.2, pred[512]{0:T(512)(128)(4,1)S(1)} %get-tuple-element.6), kind=kOutput, calls=%fused_computation.40 | convolution fusion | flops 537526272 | bytes 6554112 | tf_op jit(solution)/shard_map/dot_general | solution.py:22
  253.5 6.4 %fusion.14 = f32[2048,256]{1,0:T(8,128)} fusion(s32[]{:T(128)S(6)} %select_n.190, f32[2048,256]{1,0:T(8,128)S(1)} %convolution_subtract_fusion.1, s32[]{:T(128)S(6)} %select_n.182, s32[]{:T(128)S(6)} %select_n.184, s32[]{:T(128)S(6)} %select_n.186, s32[]{:T(128)S(6)} %select_n.188, f32[2048]{0:T(1024)S(1)} %bitcast.131, f32[2048]{0:T(1024)S(1)} %bitcast.135, ...), kind=kLoop, calls=%fused_computation.60 | loop fusion | flops 7340032 | bytes 4235284 | tf_op jit(solution)/shard_map/add | solution.py:16
  259.9 3.1 %gather_fusion.3 = bf16[512,256]{1,0:T(8,128)(2,1)S(1)} fusion(f32[2048,256]{1,0:T(8,128)} %fusion.14, s32[1024]{0:T(1024)S(1)} %pad_clamp_fusion.1), kind=kCustom, calls=%fused_computation.4.clone | custom fusion | bytes 526336 | tf_op jit(solution)/shard_map/jit(_take)/gather | solution.py:19
  263.1 3.7 %fusion.2 = f32[1,2048,256]{2,1,0:T(8,128)} fusion(f32[2048,256]{1,0:T(8,128)} %fusion.1, f32[2048,256]{1,0:T(8,128)} %fusion.14, bf16[2048,512]{1,0:T(8,128)(2,1)S(1)} %bitcast.123, pred[]{:T(512)S(6)} %ge.18, bf16[512,256]{1,0:T(8,128)(2,1)S(1)} %gather_fusion.3, pred[512]{0:T(512)(128)(4,1)S(1)} %get-tuple-element.9), kind=kOutput, calls=%fused_computation.44 | convolution fusion | flops 538050560 | bytes 8651265 | tf_op jit(solution)/shard_map/dot_general | solution.py:22
  (22 shorter events, 0.2 us)
Async XLA Ops:
  3.3 4.4 %copy-start.1 = (s32[1,1,512]{2,1,0:T(1,128)S(1)}, s32[1,1,512]{2,1,0:T(1,128)}, u32[]{:S(2)}) copy-start(s32[1,1,512]{2,1,0:T(1,128)} %param.18) | copy-start | bytes 6148
  3.3 9.2 %copy-start = (f32[5,2048]{1,0:T(8,128)S(1)}, f32[5,2048]{1,0:T(8,128)}, u32[]{:S(2)}) copy-start(f32[5,2048]{1,0:T(8,128)} %param.15) | copy-start | bytes 122884
  3.3 9.3 %copy-start.2 = (s32[5]{0:T(128)S(1)}, s32[5]{0:T(128)}, u32[]{:S(2)}) copy-start(s32[5]{0:T(128)} %param.14) | copy-start | bytes 64
  3.3 31.6 %all-to-all-start = ((bf16[8,1,256,512]{3,2,1,0:T(8,128)(2,1)}), bf16[8,1,256,512]{3,2,1,0:T(8,128)(2,1)S(1)}, u32[]{:S(2)}, u32[]{:S(2)}) async-start(bf16[8,1,256,512]{3,2,1,0:T(8,128)(2,1)} %stack.5), calls=%async_computation | async-start | bytes 4194304 | tf_op jit(solution)/shard_map/all_to_all | solution.py:44
  7.7 39.8 %collective-permute-start.3 = (s32[1,512]{1,0:T(1,128)S(1)}, s32[1,512]{1,0:T(1,128)S(1)}, u32[]{:S(2)}, u32[]{:S(2)}) collective-permute-start(s32[1,512]{1,0:T(1,128)S(1)} %bitcast.145), channel_id=1, source_target_pairs={{0,8},{8,16},{16,24},{24,32},{32,40},{40,48},{48,56},{56,64},{64,7... | collective-permute-start | bytes 6152 | tf_op jit(solution)/shard_map/ppermute | solution.py:10
  34.9 8.4 %copy-start.3 = (f32[1,1,512]{2,1,0:T(1,128)S(1)}, f32[1,1,512]{2,1,0:T(1,128)}, u32[]{:S(2)}) copy-start(f32[1,1,512]{2,1,0:T(1,128)} %param.19) | copy-start | bytes 6148
  38.7 63.4 %collective-permute-start = (f32[2048,256]{1,0:T(8,128)}, f32[2048,256]{1,0:T(8,128)}, u32[]{:S(2)}, u32[]{:S(2)}) collective-permute-start(f32[2048,256]{1,0:T(8,128)} %convolution_subtract_fusion.3), channel_id=1, source_target_pairs={{0,8},{8,16},{16,24},{24,32},{32,40},{40,48},{48,56},{56,64},{64,7... | collective-permute-start | bytes 6291464 | tf_op jit(solution)/shard_map/ppermute | solution.py:10
  44.0 44.4 %collective-permute-start.4 = (f32[2048,1]{0,1:T(1,128)S(1)}, f32[2048,1]{0,1:T(1,128)S(1)}, u32[]{:S(2)}, u32[]{:S(2)}) collective-permute-start(f32[2048,1]{0,1:T(1,128)S(1)} %fusion.11), channel_id=1, source_target_pairs={{0,8},{8,16},{16,24},{24,32},{32,40},{40,48},{48,56},{56,64},{64,7... | collective-permute-start | bytes 24584 | tf_op jit(solution)/shard_map/ppermute | solution.py:10
  92.4 9.7 %collective-permute-start.5 = (f32[2048,1]{0,1:T(1,128)S(1)}, f32[2048,1]{0,1:T(1,128)S(1)}, u32[]{:S(2)}, u32[]{:S(2)}) collective-permute-start(f32[2048,1]{0,1:T(1,128)S(1)} %fusion.10), channel_id=1, source_target_pairs={{0,16},{8,24},{16,32},{24,40},{32,48},{40,56},{48,64},{56,72},{64,... | collective-permute-start | bytes 24584 | tf_op jit(solution)/shard_map/ppermute | solution.py:10
  97.8 94.5 %collective-permute-start.2 = (bf16[1,2048,512]{2,1,0:T(8,128)(2,1)S(1)}, bf16[1,2048,512]{2,1,0:T(8,128)(2,1)}, u32[]{:S(2)}, u32[]{:S(2)}) collective-permute-start(bf16[1,2048,512]{2,1,0:T(8,128)(2,1)S(1)} %bitcast.120), channel_id=1, source_target_pairs={{0,8},{8,16},{16,24},{24,32},{32,40},{40,48},{48,56},{56,64},{64,7... | collective-permute-start | bytes 6291464 | tf_op jit(solution)/shard_map/ppermute | solution.py:10
  115.6 123.4 %collective-permute-start.1 = (f32[2048,256]{1,0:T(8,128)}, f32[2048,256]{1,0:T(8,128)}, u32[]{:S(2)}, u32[]{:S(2)}) collective-permute-start(f32[2048,256]{1,0:T(8,128)} %fusion.1), channel_id=1, source_target_pairs={{0,16},{8,24},{16,32},{24,40},{32,48},{40,56},{48,64},{56,72},{64,... | collective-permute-start | bytes 6291464 | tf_op jit(solution)/shard_map/ppermute | solution.py:10
